TPU v7x, 128 devices: a whole 4x4x4 slice. The times are simulated.
128 devices in a mesh: ex: 16 (over y, x), ey: 8 (over z, core).
Axes of the slice: x: 4, y: 4, z: 4, core: 2. Of those that a mesh axis runs over, the one named last changes fastest.
Arguments:
- tokens: bfloat16 [8192, 3584], P(('ex', 'ey')), may hold values from -6 to 6
- route_ids: int32 [8192, 8], P(('ex', 'ey')), may hold values from 0 to 127, all different within a row; in each aligned block of 64 rows (0 to 63, 64 to 127, ...) at most 8 rows name the same one
- route_weight: bfloat16 [8192, 8], P(('ex', 'ey')), may hold values from 0.19921875 to 1
- w_gate: bfloat16 [128, 3584, 1024], P(('ex', 'ey')), may hold values from -0.09375 to 0.09375
- w_up: bfloat16 [128, 3584, 1024], P(('ex', 'ey')), may hold values from -0.09375 to 0.09375
- w_down: bfloat16 [128, 1024, 3584], P(('ex', 'ey')), may hold values from -0.1875 to 0.1875
- shared_gate: bfloat16 [3584, 2048], P(None, 'ex'), may hold values from -0.09375 to 0.09375
- shared_up: bfloat16 [3584, 2048], P(None, 'ex'), may hold values from -0.09375 to 0.09375
- shared_down: bfloat16 [2048, 3584], P('ex'), may hold values from -0.125 to 0.125
Outputs:
- layer_out: bfloat16 [8192, 3584], P(('ex', 'ey'))
Inputs may be any that keep to these rules, and one draw needn't show every extreme that they name: `route_ids`: each row names 8 different experts; within the rows of one device no expert is named more than 8 times, a bound that some block reaches.
All inputs are finite; a program needn't handle non-finite values.
Results may differ from a plain program's by a relative error of at most 0.009.
Values may be sent and summed in bfloat16 or wider, within the bound.
A program may use at most 128 MiB of HBM per device.

v0:
```python
import jax
import jax.numpy as jnp
from jax import lax
from jax.sharding import PartitionSpec as P


def swiglu(chosen, gate_weight, up_weight, down_weight):
    gate_act = jnp.dot(chosen, gate_weight, preferred_element_type=jnp.float32)
    up_act = jnp.dot(chosen, up_weight, preferred_element_type=jnp.float32)
    hidden = (jax.nn.silu(gate_act) * up_act).astype(jnp.bfloat16)
    return jnp.dot(hidden, down_weight, preferred_element_type=jnp.float32)


def shared_expert(tokens, shared_gate, shared_up, shared_down):
    gathered = lax.all_gather(tokens, "ex", axis=0, tiled=True)
    return lax.psum_scatter(
        swiglu(gathered, shared_gate, shared_up, shared_down).astype(jnp.bfloat16),
        "ex",
        scatter_dimension=0,
        tiled=True,
    ).astype(jnp.float32)


def shards(
    tokens, route_ids, route_weight, w_gate, w_up, w_down, shared_gate, shared_up, shared_down
):
    tok_rows = tokens.shape[0]
    top_count = route_ids.shape[1]
    width = tokens.shape[1]
    experts = lax.axis_size("ex") * lax.axis_size("ey")
    slot_most = max(2, 2 * tok_rows * top_count // experts)
    capacity = experts * slot_most
    flat_ids = route_ids.reshape(-1)
    onehot = (flat_ids[:, None] == jnp.arange(experts, dtype=jnp.int32)[None, :]).astype(jnp.int32)
    slot_rank = jnp.sum((jnp.cumsum(onehot, axis=0) - onehot) * onehot, axis=1)
    slot_place = flat_ids * slot_most + slot_rank
    matches = (slot_place[:, None] == jnp.arange(capacity, dtype=jnp.int32)[None, :]).astype(
        jnp.float32
    )
    matches = matches.reshape(tok_rows, top_count, capacity)
    placing = jnp.sum(matches, axis=1).astype(jnp.bfloat16)
    combine_mat = jnp.sum(matches * route_weight.astype(jnp.float32)[:, :, None], axis=1).astype(
        jnp.bfloat16
    )
    outgoing = jnp.einsum("tc,td->cd", placing, tokens, preferred_element_type=jnp.float32).astype(
        jnp.bfloat16
    )
    outgoing = outgoing.reshape(experts, slot_most, width)
    by_group = outgoing.reshape(lax.axis_size("ex"), lax.axis_size("ey"), slot_most, width)
    arrived = lax.all_to_all(
        lax.all_to_all(by_group, "ex", split_axis=0, concat_axis=0, tiled=True),
        "ey",
        split_axis=1,
        concat_axis=1,
        tiled=True,
    )
    layout = arrived.shape
    result = swiglu(arrived.reshape(-1, width), w_gate[0], w_up[0], w_down[0])
    produced = result.astype(jnp.bfloat16).reshape(layout)
    returned = lax.all_to_all(
        lax.all_to_all(produced, "ex", split_axis=0, concat_axis=0, tiled=True),
        "ey",
        split_axis=1,
        concat_axis=1,
        tiled=True,
    )
    returned = returned.reshape(capacity, width)
    routed = jnp.dot(combine_mat, returned, preferred_element_type=jnp.float32)
    shared = shared_expert(tokens, shared_gate, shared_up, shared_down)
    return (shared + routed).astype(jnp.bfloat16)


def solution(mesh):
    in_specs = (
        P(("ex", "ey"), None),
        P(("ex", "ey"), None),
        P(("ex", "ey"), None),
        P(("ex", "ey"), None, None),
        P(("ex", "ey"), None, None),
        P(("ex", "ey"), None, None),
        P(None, "ex"),
        P(None, "ex"),
        P("ex", None),
    )
    out_specs = P(("ex", "ey"), None)
    return jax.shard_map(shards, mesh=mesh, in_specs=in_specs, out_specs=out_specs, check_vma=False)
```

profile of v0, /device:TPU:1, one launch (start us, length us, event | category | flops | bytes accessed | tf_op | source)
XLA Modules:
  0.0 516.1 jit_solution(11821766274320693262)
XLA Ops:
  6.5 0.0 copy-start
  6.5 0.9 copy.61
  7.4 0.1 eq.43
  7.5 0.1 eq.39
  7.6 0.8 copy.67
  8.3 0.1 copy.63
  8.5 0.2 fusion.16
  8.8 0.2 fusion.15
  9.0 0.1 reduce_sum.30
  9.1 0.1 copy.65
  9.2 0.7 multiply_add_fusion
  9.9 0.1 copy.66
  10.0 1.3 select_reduce_fusion
  11.3 6.1 %convolution_convert_fusion.1 = bf16[1024,3584]{1,0:T(8,128)(2,1)} fusion(bf16[64,3584]{1,0:T(8,128)(2,1)} %param.9, bf16[64,1024]{1,0:T(8,128)(2,1)S(1)} %get-tuple-element.6), kind=kOutput, calls=%fused_computation.1 | convolution fusion | flops 473432064 | bytes 7929856 | tf_op jit(solution)/shard_map/tc,td->cd/dot_general | solution.py:45
  17.4 7.6 %all-to-all-start = ((bf16[16,8,8,3584]{3,2,1,0:T(8,128)(2,1)}), bf16[16,8,8,3584]{3,2,1,0:T(8,128)(2,1)}, u32[]{:S(2)}, u32[]{:S(2)}) async-start(bf16[16,8,8,3584]{3,2,1,0:T(8,128)(2,1)} %bitcast.41), calls=%async_computation.1 | async-start | bytes 14680064 | tf_op jit(solution)/shard_map/all_to_all | solution.py:51
  25.0 0.0 all-gather.2.cloned.1.call-start
  25.0 0.7 all-gather.2.cloned.1.call-update
  25.7 0.0 reduce-scatter.2.cloned.1.call-start
  25.8 124.8 %all-to-all-done = bf16[16,8,8,3584]{3,2,1,0:T(8,128)(2,1)} async-done(((bf16[16,8,8,3584]{3,2,1,0:T(8,128)(2,1)}), bf16[16,8,8,3584]{3,2,1,0:T(8,128)(2,1)}, u32[]{:S(2)}, u32[]{:S(2)}) %all-to-all-start) | async-done | bytes 7340064 | tf_op jit(solution)/shard_map/all_to_all | solution.py:51
  150.5 3.9 copy.68
  154.5 92.7 %all_to_all.20 = bf16[16,8,8,3584]{3,2,0,1:T(8,128)(2,1)} all-to-all(bf16[16,8,8,3584]{3,2,0,1:T(8,128)(2,1)S(1)} %copy.68), channel_id=1, replica_groups=mesh['ex'=16,'ey'=8] {'ey'}, dimensions={1} | all-to-all | bytes 14680064 | tf_op jit(solution)/shard_map/all_to_all | solution.py:50
  247.1 3.9 copy.69
  251.0 9.9 %fusion.1 = f32[1024,1024]{1,0:T(8,128)S(1)} fusion(bf16[1024,3584]{1,0:T(8,128)(2,1)S(1)} %bitcast.42, bf16[1,3584,1024]{2,1,0:T(8,128)(2,1)} %param.13), kind=kOutput, calls=%fused_computation.4 | convolution fusion | flops 7516192768 | bytes 18874368 | tf_op jit(solution)/shard_map/dot_general | solution.py:9
  261.0 0.0 copy-start.3
  261.0 11.7 %multiply_convert_fusion = bf16[1024,1024]{1,0:T(8,128)(2,1)} fusion(f32[1024,1024]{1,0:T(8,128)S(1)} %fusion.1, bf16[1024,3584]{1,0:T(8,128)(2,1)S(1)} %bitcast.43, bf16[1,3584,1024]{2,1,0:T(8,128)(2,1)} %param.12), kind=kOutput, calls=%fused_computation.10 | convolution fusion | flops 7522484224 | bytes 20971520 | tf_op jit(solution)/shard_map/dot_general | solution.py:8
  272.6 0.0 copy-start.2
  272.6 0.0 all-gather.2.cloned.1.call-done
  272.6 0.0 copy-done.3
  272.7 5.2 %fusion.23 = f32[1024,128]{1,0:T(8,128)S(1)} fusion(bf16[1024,3584]{1,0:T(8,128)(2,1)} %all-gather.2.cloned.1.call-done, bf16[3584,128]{1,0:T(8,128)(2,1)S(1)} %copy-done.3), kind=kOutput, calls=%fused_computation.36 | convolution fusion | flops 939524096 | bytes 8781824 | tf_op jit(solution)/shard_map/dot_general | solution.py:8
  277.9 0.0 copy-done
  277.9 0.0 copy-done.2
  277.9 11.8 %convolution_convert_fusion.2 = bf16[1024,3584]{1,0:T(8,128)(2,1)} fusion(bf16[128,3584]{1,0:T(8,128)(2,1)S(1)} %copy-done, bf16[1024,3584]{1,0:T(8,128)(2,1)} %all-gather.2.cloned.1.call-done, bf16[3584,128]{1,0:T(8,128)(2,1)S(1)} %copy-done.2, f32[1024,128]{1,0:T(8,128)S(1)} %fusion.23), kind=kOutput, calls=%fused_computation.2 | convolution fusion | flops 1883504640 | bytes 17039360 | tf_op jit(solution)/shard_map/dot_general | solution.py:11
  289.7 0.0 copy-start.4
  289.7 0.0 reduce-scatter.2.cloned.1.call-update
  289.8 1.6 copy-done.4
  291.3 11.3 %convolution_convert_fusion = bf16[1024,3584]{1,0:T(8,128)(2,1)S(1)} fusion(bf16[1024,1024]{1,0:T(8,128)(2,1)S(1)} %copy-done.4, bf16[1,1024,3584]{2,1,0:T(8,128)(2,1)} %param.14), kind=kOutput, calls=%fused_computation | convolution fusion | flops 7519862784 | bytes 16777216 | tf_op jit(solution)/shard_map/dot_general | solution.py:11
  302.6 105.1 %all_to_all.21 = bf16[16,8,8,3584]{3,2,1,0:T(8,128)(2,1)S(1)} all-to-all(bf16[16,8,8,3584]{3,2,1,0:T(8,128)(2,1)S(1)} %bitcast.44), channel_id=1, replica_groups=mesh['ex'=16,'ey'=8] {'ex'}, dimensions={0} | all-to-all | bytes 14680064 | tf_op jit(solution)/shard_map/all_to_all | solution.py:61
  407.7 3.7 copy.70
  411.4 88.8 %all_to_all.22 = bf16[16,8,8,3584]{3,2,0,1:T(8,128)(2,1)S(1)} all-to-all(bf16[16,8,8,3584]{3,2,0,1:T(8,128)(2,1)} %copy.70), channel_id=1, replica_groups=mesh['ex'=16,'ey'=8] {'ey'}, dimensions={1} | all-to-all | bytes 14680064 | tf_op jit(solution)/shard_map/all_to_all | solution.py:60
  500.3 0.0 copy-start.1
  500.3 3.8 copy.71
  504.0 0.0 reduce-scatter.2.cloned.1.call-done
  504.0 5.3 %fusion.5 = bf16[64,3584]{1,0:T(8,128)(2,1)} fusion(bf16[1024,3584]{1,0:T(8,128)(2,1)} %bitcast.40, bf16[64,3584]{1,0:T(8,128)(2,1)} %reduce-scatter.2.cloned.1.call-done, bf16[64,1024]{1,0:T(8,128)(2,1)S(1)} %get-tuple-element.5), kind=kOutput, calls=%fused_computation.9 | convolution fusion | flops 470450176 | bytes 8388608 | tf_op jit(solution)/shard_map/dot_general | solution.py:68
  509.3 0.0 copy-done.1
  (6 shorter events, 0.1 us)
Async XLA Ops:
  6.5 271.3 %copy-start = (bf16[128,3584]{1,0:T(8,128)(2,1)S(1)}, bf16[128,3584]{1,0:T(8,128)(2,1)}, u32[]{:S(2)}) copy-start(bf16[128,3584]{1,0:T(8,128)(2,1)} %param.17) | copy-start | bytes 2752516
  17.4 133.2 %all-to-all-start = ((bf16[16,8,8,3584]{3,2,1,0:T(8,128)(2,1)}), bf16[16,8,8,3584]{3,2,1,0:T(8,128)(2,1)}, u32[]{:S(2)}, u32[]{:S(2)}) async-start(bf16[16,8,8,3584]{3,2,1,0:T(8,128)(2,1)} %bitcast.41), calls=%async_computation.1 | async-start | bytes 14680064 | tf_op jit(solution)/shard_map/all_to_all | solution.py:51
  25.0 247.7 %all-gather.2.cloned.1.call-start = ((), (), s32[]{:S(2)}) async-start(), calls=%async_computation.5 | async-start | bytes 7798784 | tf_op jit(solution)/shard_map/all_gather | solution.py:15
  25.7 478.3 %reduce-scatter.2.cloned.1.call-start = ((), (), s32[]{:S(2)}) async-start(), calls=%async_computation.6 | async-start | bytes 7798784 | tf_op jit(solution)/shard_map/reduce_scatter | solution.py:16
  261.0 11.7 %copy-start.3 = (bf16[3584,128]{1,0:T(8,128)(2,1)S(1)}, bf16[3584,128]{1,0:T(8,128)(2,1)}, u32[]{:S(2)}) copy-start(bf16[3584,128]{1,0:T(8,128)(2,1)} %param.15) | copy-start | bytes 2752516
  272.6 5.2 %copy-start.2 = (bf16[3584,128]{1,0:T(8,128)(2,1)S(1)}, bf16[3584,128]{1,0:T(8,128)(2,1)}, u32[]{:S(2)}) copy-start(bf16[3584,128]{1,0:T(8,128)(2,1)} %param.16) | copy-start | bytes 2752516
  289.7 1.6 copy-start.4
  500.3 9.0 %copy-start.1 = (bf16[128,3584]{1,0:T(8,128)(2,1)S(1)}, bf16[128,3584]{1,0:T(8,128)(2,1)}, u32[]{:S(2)}) copy-start(bf16[128,3584]{1,0:T(8,128)(2,1)} %param.17) | copy-start | bytes 2752516
Sparse Core Ops, SparseCore 0:
  27.9 138.8 all-gather.1
  289.9 148.8 reduce-scatter.1
where the time goes:
time: 517 us; the launch traced here: 516 us
  blocking collectives  287 us (56%)
  waiting for transfers between devices  125 us (24%)
  matrix products  61.3 us (12%)
  local copies, waits for them, and re-layouts  19 us (4%)
  between operations  13.5 us (3%)
  starting transfers between devices  7.69 us (1%)
    all_to_all x1, waiting for transfers between devices, shards(): lax.all_to_all(by_group, 'ex', split_axis=0, concat_axis=0, tiled=True)  125 us
    all_to_all x1, blocking collectives, shards(): lax.all_to_all(produced, 'ex', split_axis=0, concat_axis=0, tiled=True)  105 us
    all_to_all x1, blocking collectives, shards(): lax.all_to_all(lax.all_to_all(by_group, 'ex', split_axis=0, concat_axis=0...  92.7 us
    all_to_all x1, blocking collectives, shards(): lax.all_to_all(lax.all_to_all(produced, 'ex', split_axis=0, concat_axis=0...  88.8 us
    dot_general x2, matrix products, swiglu(): return jnp.dot(hidden, down_weight, preferred_element_type=jnp.float32)  23.1 us
    dot_general x2, matrix products, swiglu(): gate_act = jnp.dot(chosen, gate_weight, preferred_element_type=jnp.float32)  16.9 us
  transfers between devices with their start and end apart: 3, of which 1 were waited for; matrix products, arithmetic and copies ran while one was open for 9% of the time, Pallas kernels for 0%

commit v1 on v0

v1 whole, which is shorter than its diff:
```python
import functools

import jax
import jax.numpy as jnp
from jax import lax
from jax.experimental import pallas as pl
from jax.experimental.pallas import tpu as pltpu
from jax.sharding import PartitionSpec as P

MESH = pl.DeviceIdType.MESH
F32 = jnp.float32
BF16 = jnp.bfloat16
LAG = 2
W = 256


def dot(a, b):
    return jnp.dot(a, b, preferred_element_type=F32)


class Place:
    def __init__(self):
        self.ex = lax.axis_index("ex")
        self.ey = lax.axis_index("ey")
        self.x = lax.rem(self.ex, 4)
        self.y = lax.div(self.ex, 4)

    def along_x(self, step):
        return (self.y * 4 + lax.rem(self.x + step, 4), self.ey)

    def along_y(self, step):
        return (lax.rem(self.y + step, 4) * 4 + self.x, self.ey)

    def along_ey(self, step):
        return (self.ex, lax.rem(self.ey + step, 8))

    def greet(self):
        barrier = pltpu.get_barrier_semaphore()
        partners = [self.along_x(s) for s in (1, 2, 3)]
        partners += [self.along_y(s) for s in (1, 2, 3)]
        partners += [self.along_ey(s) for s in range(1, 8)]
        for partner in partners:
            pl.semaphore_signal(barrier, inc=1, device_id=partner, device_id_type=MESH)
        pl.semaphore_wait(barrier, len(partners))


def remote(src, dst, send, recv, partner):
    return pltpu.make_async_remote_copy(
        src_ref=src, dst_ref=dst, send_sem=send, recv_sem=recv, device_id=partner, device_id_type=MESH
    )


def dispatch_kernel(
    pairs,
    tok, ids, weight, w_gate, w_up, s_gate, s_up,
    h_out, hs_out, comb,
    ag, snd, rcv, acc_g, acc_u, gate_v, up_v, sgu, meta, metas, place_t, acc_s,
    load_sem, m1_send, m1_recv, m2_send, m2_recv, p1_send, p1_recv, p2_send, p2_recv, z_send, z_recv,
):
    at = Place()
    x, y, ey = at.x, at.y, at.ey

    def loads(i):
        rows = pl.ds(pl.multiple_of(i * 2 * W, 2 * W), 2 * W)
        return (
            pltpu.make_async_copy(w_gate.at[0, rows], gate_v.at[i], load_sem.at[0, i]),
            pltpu.make_async_copy(w_up.at[0, rows], up_v.at[i], load_sem.at[1, i]),
            pltpu.make_async_copy(s_gate.at[rows], sgu.at[i, :, pl.ds(0, 128)], load_sem.at[2, i]),
            pltpu.make_async_copy(s_up.at[rows], sgu.at[i, :, pl.ds(128, 128)], load_sem.at[3, i]),
        )

    def start_loads(i, carry):
        for copy in loads(i):
            copy.start()
        return carry

    lax.fori_loop(0, pairs, start_loads, 0)

    lane = lax.broadcasted_iota(jnp.int32, (64, 128), 1)
    hits = [ids[:, k : k + 1] == lane for k in range(8)]
    named = sum(jnp.where(hit, 1.0, 0.0) for hit in hits)
    lower = lax.broadcasted_iota(jnp.int32, (64, 64), 0) > lax.broadcasted_iota(jnp.int32, (64, 64), 1)
    before = dot(jnp.where(lower, 1.0, 0.0).astype(BF16), named.astype(BF16))
    info = jnp.zeros((64, 128), F32)
    for k in range(8):
        rank = jnp.sum(jnp.where(hits[k], before, 0.0), axis=1, keepdims=True)
        code = ids[:, k : k + 1].astype(F32) * 32.0 + rank
        info = jnp.where(lane == k, code, info)
        info = jnp.where(lane == 8 + k, weight[:, k : k + 1].astype(F32), info)
    meta[...] = info
    metas[y, x] = info

    def own(c, carry):
        columns = pl.ds(pl.multiple_of(c * W, W), W)
        ag[c, y, x] = tok[:, columns]
        return carry

    lax.fori_loop(0, 2 * pairs, own, 0)

    at.greet()

    def first(c, half, s):
        partner = at.along_x(s) if half == 0 else at.along_y(s)
        columns = pl.ds(pl.multiple_of(c * W, W), W)
        return remote(tok.at[:, columns], ag.at[c, y, x], p1_send.at[c, s - 1], p1_recv.at[c, s - 1], partner)

    def second(c, half, s):
        if half == 0:
            return remote(ag.at[c, y], ag.at[c, y], p2_send.at[c, s - 1], p2_recv.at[c, s - 1], at.along_y(s))
        return remote(ag.at[c, :, x], ag.at[c, :, x], p2_send.at[c, s - 1], p2_recv.at[c, s - 1], at.along_x(s))

    def cross(c, s):
        target = lax.rem(ey + s, 8)
        return remote(snd.at[c, target], rcv.at[c, ey], z_send.at[c, s - 1], z_recv.at[c, s - 1], at.along_ey(s))

    def meta_first(s):
        return remote(meta, metas.at[y, x], m1_send.at[s - 1], m1_recv.at[s - 1], at.along_x(s))

    def meta_second(s):
        return remote(metas.at[y], metas.at[y], m2_send.at[s - 1], m2_recv.at[s - 1], at.along_y(s))

    def start_first(i):
        for half in (0, 1):
            for s in (2, 1, 3):
                first(2 * i + half, half, s).start()

    def start_second(i):
        for half in (0, 1):
            for s in (1, 2, 3):
                first(2 * i + half, half, s).wait_recv()
            for s in (2, 1, 3):
                second(2 * i + half, half, s).start()

    for s in (2, 1, 3):
        meta_first(s).start()
    start_first(0)
    start_first(1)
    for s in (1, 2, 3):
        meta_first(s).wait_recv()
    for s in (2, 1, 3):
        meta_second(s).start()
    start_second(0)

    def clear(r, carry):
        rows = pl.ds(pl.multiple_of(r * 64, 64), 64)
        acc_g[rows] = jnp.zeros((64, 1024), F32)
        acc_u[rows] = jnp.zeros((64, 1024), F32)
        acc_s[rows] = jnp.zeros((64, 256), F32)
        return carry

    lax.fori_loop(0, 16, clear, 0)

    for s in (1, 2, 3):
        meta_second(s).wait_recv()

    def matrices(q, carry):
        known = metas[q].reshape(256, 128)
        slot = lax.broadcasted_iota(jnp.int32, (256, 256), 1).astype(F32)
        source = lax.div(lax.broadcasted_iota(jnp.int32, (256, 1), 0), 64)
        shift = (source * 8 - at.ex * 256).astype(F32)
        total = jnp.zeros((256, 256), F32)
        for k in range(8):
            hit = (known[:, k : k + 1] + shift) == slot
            total = jnp.where(hit, known[:, 8 + k : 9 + k], total)
        comb[q] = total.astype(BF16)
        place_t[q] = jnp.where(total > 0.0, 1.0, 0.0).T.astype(BF16)
        return carry

    lax.fori_loop(0, 4, matrices, 0)

    def compact(i):
        for half in (0, 1):
            c = 2 * i + half
            for s in (1, 2, 3):
                second(c, half, s).wait_recv()

            def quad(q, carry):
                rows = dot(place_t[q], ag[c, q].reshape(256, W)).astype(BF16)
                snd[c, :, pl.ds(pl.multiple_of(q * 32, 32), 32)] = rows.reshape(8, 32, W)
                return carry

            lax.fori_loop(0, 4, quad, 0)
            rcv[c, ey] = snd[c, ey]
            for s in (4, 3, 5, 2, 6, 1, 7):
                cross(c, s).start()

    def shared(i):
        for copy in loads(i)[2:]:
            copy.wait()

        def quad(q, carry):
            rows = pl.ds(pl.multiple_of(q * 256, 256), 256)
            acc_s[rows] += dot(ag[2 * i, q].reshape(256, W), sgu[i, :W]) + dot(
                ag[2 * i + 1, q].reshape(256, W), sgu[i, W:]
            )
            return carry

        lax.fori_loop(0, 4, quad, 0)

    def expert(i):
        for copy in loads(i)[:2]:
            copy.wait()
        for half in (0, 1):
            for s in range(1, 8):
                cross(2 * i + half, s).wait_recv()

        def tile(m, carry):
            rows = pl.ds(pl.multiple_of(m * 256, 256), 256)
            blocks = pl.ds(2 * m, 2)
            left = rcv[2 * i, blocks].reshape(256, W)
            right = rcv[2 * i + 1, blocks].reshape(256, W)
            acc_g[rows] += dot(left, gate_v[i, :W]) + dot(right, gate_v[i, W:])
            acc_u[rows] += dot(left, up_v[i, :W]) + dot(right, up_v[i, W:])
            return carry

        lax.fori_loop(0, 4, tile, 0)

    def step(i, carry):
        @pl.when(i + 2 < pairs)
        def _():
            start_first(i + 2)

        @pl.when(i + 1 < pairs)
        def _():
            start_second(i + 1)

        @pl.when(i < pairs)
        def _():
            compact(i)
            shared(i)

        @pl.when(i >= LAG)
        def _():
            expert(i - LAG)

        return carry

    lax.fori_loop(0, pairs + LAG, step, 0)

    def finish(r, carry):
        rows = pl.ds(pl.multiple_of(r * 64, 64), 64)
        h_out[rows] = (jax.nn.silu(acc_g[rows]) * acc_u[rows]).astype(BF16)
        both = acc_s[rows]
        hs_out[rows] = (jax.nn.silu(both[:, :128]) * both[:, 128:]).astype(BF16)
        return carry

    lax.fori_loop(0, 16, finish, 0)

    for s in (1, 2, 3):
        meta_first(s).wait_send()
        meta_second(s).wait_send()

    def drain(i, carry):
        for half in (0, 1):
            c = 2 * i + half
            for s in (1, 2, 3):
                first(c, half, s).wait_send()
                second(c, half, s).wait_send()
            for s in range(1, 8):
                cross(c, s).wait_send()
        return carry

    lax.fori_loop(0, pairs, drain, 0)


def return_kernel(
    pairs,
    h, hs, comb, w_down, s_down,
    out,
    down_v, sd_v, snd, rcv, part, got1, half_sum, got2,
    load_sem, z_send, z_recv, r1_send, r1_recv, r2_send, r2_recv,
):
    at = Place()
    x, y, ey = at.x, at.y, at.ey

    def loads(i):
        columns = pl.ds(pl.multiple_of(i * 2 * W, 2 * W), 2 * W)
        return (
            pltpu.make_async_copy(w_down.at[0, :, columns], down_v.at[i], load_sem.at[0, i]),
            pltpu.make_async_copy(s_down.at[:, columns], sd_v.at[i], load_sem.at[1, i]),
        )

    def start_loads(i, carry):
        for copy in loads(i):
            copy.start()
        return carry

    lax.fori_loop(0, pairs, start_loads, 0)
    at.greet()

    def cross(c, s):
        target = lax.rem(ey + s, 8)
        return remote(snd.at[c, target], rcv.at[c, ey], z_send.at[c, s - 1], z_recv.at[c, s - 1], at.along_ey(s))

    def first(c, half, s):
        if half == 0:
            src, partner = part.at[c, lax.rem(y + s, 4)], at.along_y(s)
        else:
            src, partner = part.at[c, :, lax.rem(x + s, 4)], at.along_x(s)
        return remote(src, got1.at[c, s - 1], r1_send.at[c, s - 1], r1_recv.at[c, s - 1], partner)

    def second(c, half, s):
        if half == 0:
            src, partner = half_sum.at[c, lax.rem(x + s, 4)], at.along_x(s)
        else:
            src, partner = half_sum.at[c, lax.rem(y + s, 4)], at.along_y(s)
        return remote(src, got2.at[c, s - 1], r2_send.at[c, s - 1], r2_recv.at[c, s - 1], partner)

    def down(i):
        loads(i)[0].wait()

        def tile(m, carry):
            rows = pl.ds(pl.multiple_of(m * 256, 256), 256)
            blocks = pl.ds(2 * m, 2)
            result = dot(h[rows], down_v[i]).astype(BF16)
            snd[2 * i, blocks] = result[:, :W].reshape(2, 128, W)
            snd[2 * i + 1, blocks] = result[:, W:].reshape(2, 128, W)
            return carry

        lax.fori_loop(0, 4, tile, 0)
        for half in (0, 1):
            c = 2 * i + half
            rcv[c, ey] = snd[c, ey]
            for s in (4, 3, 5, 2, 6, 1, 7):
                cross(c, s).start()

    def combine(i):
        loads(i)[1].wait()
        for half in (0, 1):
            c = 2 * i + half
            for s in range(1, 8):
                cross(c, s).wait_recv()

            def quad(q, carry):
                rows = rcv[c, :, pl.ds(pl.multiple_of(q * 32, 32), 32)].reshape(256, W)
                tokens = pl.ds(pl.multiple_of(q * 256, 256), 256)
                total = dot(comb[q], rows) + dot(hs[tokens], sd_v[i, :, half * W : half * W + W])
                part[c, q] = total.astype(BF16).reshape(4, 64, W)
                return carry

            lax.fori_loop(0, 4, quad, 0)
            for s in (2, 1, 3):
                first(c, half, s).start()

    def reduce(i):
        for half in (0, 1):
            c = 2 * i + half
            for s in (1, 2, 3):
                first(c, half, s).wait_recv()
            for b in range(4):
                mine = part[c, y, b] if half == 0 else part[c, b, x]
                total = mine.astype(F32)
                for s in range(3):
                    total += got1[c, s, b].astype(F32)
                half_sum[c, b] = total.astype(BF16)
            for s in (2, 1, 3):
                second(c, half, s).start()

    def final(i):
        for half in (0, 1):
            c = 2 * i + half
            for s in (1, 2, 3):
                second(c, half, s).wait_recv()
            total = half_sum[c, x if half == 0 else y].astype(F32)
            for s in range(3):
                total += got2[c, s].astype(F32)
            out[:, pl.ds(pl.multiple_of(c * W, W), W)] = total.astype(BF16)

    def step(i, carry):
        @pl.when(i < pairs)
        def _():
            down(i)

        @pl.when((i >= 1) & (i < pairs + 1))
        def _():
            combine(i - 1)

        @pl.when((i >= 2) & (i < pairs + 2))
        def _():
            reduce(i - 2)

        @pl.when(i >= 3)
        def _():
            final(i - 3)

        return carry

    lax.fori_loop(0, pairs + 3, step, 0)

    def drain(i, carry):
        for half in (0, 1):
            c = 2 * i + half
            for s in (1, 2, 3):
                first(c, half, s).wait_send()
                second(c, half, s).wait_send()
            for s in range(1, 8):
                cross(c, s).wait_send()
        return carry

    lax.fori_loop(0, pairs, drain, 0)


def shards(
    tokens, route_ids, route_weight, w_gate, w_up, w_down, shared_gate, shared_up, shared_down
):
    width = tokens.shape[1]
    pairs = width // (2 * W)
    n = 2 * pairs
    vmem = pl.BlockSpec(memory_space=pltpu.VMEM)
    hbm = pl.BlockSpec(memory_space=pl.ANY)
    dma = pltpu.SemaphoreType.DMA
    hidden, shared_hidden, comb = pl.pallas_call(
        functools.partial(dispatch_kernel, pairs),
        out_shape=(
            jax.ShapeDtypeStruct((1024, 1024), BF16),
            jax.ShapeDtypeStruct((1024, 128), BF16),
            jax.ShapeDtypeStruct((4, 256, 256), BF16),
        ),
        in_specs=[vmem] * 3 + [hbm] * 4,
        out_specs=(vmem, vmem, vmem),
        scratch_shapes=[
            pltpu.VMEM((n, 4, 4, 64, W), BF16),
            pltpu.VMEM((n, 8, 128, W), BF16),
            pltpu.VMEM((n, 8, 128, W), BF16),
            pltpu.VMEM((1024, 1024), F32),
            pltpu.VMEM((1024, 1024), F32),
            pltpu.VMEM((pairs, 2 * W, 1024), BF16),
            pltpu.VMEM((pairs, 2 * W, 1024), BF16),
            pltpu.VMEM((pairs, 2 * W, 256), BF16),
            pltpu.VMEM((64, 128), F32),
            pltpu.VMEM((4, 4, 64, 128), F32),
            pltpu.VMEM((4, 256, 256), BF16),
            pltpu.VMEM((1024, 256), F32),
            dma((4, pairs)),
            dma((3,)), dma((3,)), dma((3,)), dma((3,)),
            dma((n, 3)), dma((n, 3)), dma((n, 3)), dma((n, 3)), dma((n, 7)), dma((n, 7)),
        ],
        compiler_params=pltpu.CompilerParams(
            collective_id=0, has_side_effects=True, vmem_limit_bytes=60 * 2**20
        ),
        name="dispatch",
    )(tokens, route_ids, route_weight, w_gate, w_up, shared_gate, shared_up)
    return pl.pallas_call(
        functools.partial(return_kernel, pairs),
        out_shape=jax.ShapeDtypeStruct((64, width), BF16),
        in_specs=[vmem] * 3 + [hbm] * 2,
        out_specs=vmem,
        scratch_shapes=[
            pltpu.VMEM((pairs, 1024, 2 * W), BF16),
            pltpu.VMEM((pairs, 128, 2 * W), BF16),
            pltpu.VMEM((n, 8, 128, W), BF16),
            pltpu.VMEM((n, 8, 128, W), BF16),
            pltpu.VMEM((n, 4, 4, 64, W), BF16),
            pltpu.VMEM((n, 3, 4, 64, W), BF16),
            pltpu.VMEM((n, 4, 64, W), BF16),
            pltpu.VMEM((n, 3, 64, W), BF16),
            dma((2, pairs)),
            dma((n, 7)), dma((n, 7)), dma((n, 3)), dma((n, 3)), dma((n, 3)), dma((n, 3)),
        ],
        compiler_params=pltpu.CompilerParams(
            collective_id=1, has_side_effects=True, vmem_limit_bytes=60 * 2**20
        ),
        name="bring_back",
    )(hidden, shared_hidden, comb, w_down, shared_down)


def solution(mesh):
    in_specs = (
        P(("ex", "ey"), None),
        P(("ex", "ey"), None),
        P(("ex", "ey"), None),
        P(("ex", "ey"), None, None),
        P(("ex", "ey"), None, None),
        P(("ex", "ey"), None, None),
        P(None, "ex"),
        P(None, "ex"),
        P("ex", None),
    )
    out_specs = P(("ex", "ey"), None)
    return jax.shard_map(shards, mesh=mesh, in_specs=in_specs, out_specs=out_specs, check_vma=False)
```

time: 517 us -> 225 us (0.44)
  blocking collectives: 287 us -> 0 us
  Pallas kernels: 0 us -> 220 us
  waiting for transfers between devices: 125 us -> 0 us
  matrix products: 61.3 us -> 0 us
  local copies, waits for them, and re-layouts: 19 us -> 4.56 us
  between operations: 13.5 us -> 0.02 us
  starting transfers between devices: 7.69 us -> 0 us
    all_to_all x3 -> x0, blocking collectives: 287 us -> none  [the longest x1 105 us: shards(): lax.all_to_all(produced, 'ex', split_axis=0, concat_axis=0, tiled=True)]
    pallas_call x0 -> x2, Pallas kernels: none -> 220 us  [the longest x1 117 us: shards(): pl.pallas_call(functools.partial(dispatch_kernel, pairs), out_shape=(jax....]
    all_to_all x1 -> x0, waiting for transfers between devices: 125 us -> none  [shards(): lax.all_to_all(by_group, 'ex', split_axis=0, concat_axis=0, tiled=True)]
    dot_general x7 -> x0, matrix products: 61.3 us -> none  [the longest x2 23.1 us: swiglu(): return jnp.dot(hidden, down_weight, preferred_element_type=jnp.float32)]
    all_to_all x4 -> x0, local copies, waits for them, and re-layouts: 15.2 us -> none  [the longest x1 3.92 us: shards(): lax.all_to_all(by_group, 'ex', split_axis=0, concat_axis=0, tiled=True)]
    all_to_all x1 -> x0, starting transfers between devices: 7.61 us -> none  [shards(): lax.all_to_all(by_group, 'ex', split_axis=0, concat_axis=0, tiled=True)]
  transfers between devices with their start and end apart: 3 -> 0, of which waited for: 1 -> 0; matrix products, arithmetic and copies ran while one was open for 9% -> 0% of each run, Pallas kernels for 0% -> 0%
where the time goes in v1:
time: 225 us
  Pallas kernels  220 us (98%)
  local copies, waits for them, and re-layouts  4.56 us (2%)
    pallas_call x1, Pallas kernels, shards(): pl.pallas_call(functools.partial(dispatch_kernel, pairs), out_shape=(jax....  117 us
    pallas_call x1, Pallas kernels, shards(): pl.pallas_call(functools.partial(return_kernel, pairs), out_shape=jax.Sha...  103 us
    unnamed x3, local copies, waits for them, and re-layouts  4.56 us

profile of v1, /device:TPU:1, one launch (start us, length us, event | category | flops | bytes accessed | tf_op | source)
XLA Modules:
  0.0 224.6 jit_solution(12692175114109770360)
XLA Ops:
  0.0 1.4 copy.11.weight
  1.4 1.4 copy.10.ids
  2.7 117.2 %dispatch.1 = (bf16[1024,1024]{1,0:T(8,128)(2,1)}, bf16[1024,128]{1,0:T(8,128)(2,1)}, bf16[4,256,256]{2,1,0:T(8,128)(2,1)}) custom-call(bf16[64,3584]{1,0:T(8,128)(2,1)} %tok.1, s32[64,8]{1,0:T(8,128)} %copy.10.ids, bf16[64,8]{1,0:T(8,128)(2,1)} %copy.11.weight, bf16[1,3584,1024]{2,1,0:T(8,128)(2,1)} %w_gate.1, bf16[1,3584,1024]{2,1,0:T(8,128)(2,1)} %w_up.1, ...), custom_call_target="tpu_custom_call" | custom-call | tf_op jit(solution)/shard_map/dispatch/pallas_call | solution.py:412
  119.9 102.8 %bring_back.1 = bf16[64,3584]{1,0:T(8,128)(2,1)} custom-call(bf16[1024,1024]{1,0:T(8,128)(2,1)} %get-tuple-element.8.h, bf16[1024,128]{1,0:T(8,128)(2,1)} %get-tuple-element.9.hs, bf16[4,256,256]{2,1,0:T(8,128)(2,1)} %get-tuple-element.10.comb, bf16[1,1024,3584]{2,1,0:T(8,128)(2,1)} %w_down.1, bf16[128,3584]{1,0:T(8,128)(2,1)} %s_down.1), custom_call_target="tpu_custom_call" | custom-call | tf_op jit(solution)/shard_map/bring_back/pallas_call | solution.py:443
  222.8 1.8 copy.13

commit v2 on v1

v2 whole, which is shorter than its diff:
```python
import functools

import jax
import jax.numpy as jnp
from jax import lax
from jax.experimental import pallas as pl
from jax.experimental.pallas import tpu as pltpu
from jax.sharding import PartitionSpec as P

MESH = pl.DeviceIdType.MESH
F32 = jnp.float32
BF16 = jnp.bfloat16
LAG = 2
W = 256


def dot(a, b):
    return jnp.dot(a, b, preferred_element_type=F32)


NEAR = ((0, 0), (0, 1), (1, 0), (1, 1), (3, 0), (3, 1))
FAR = tuple((dy, dc) for dy in range(4) for dc in range(2))


class Place:
    def __init__(self):
        self.ex = lax.axis_index("ex")
        self.ey = lax.axis_index("ey")
        self.x = lax.rem(self.ex, 4)
        self.y = lax.div(self.ex, 4)
        self.z = lax.div(self.ey, 2)
        self.c = lax.rem(self.ey, 2)

    def at(self, dx, dy, dz, dc):
        ex = lax.rem(self.y + dy, 4) * 4 + lax.rem(self.x + dx, 4)
        ey = lax.rem(self.z + dz, 4) * 2 + lax.rem(self.c + dc, 2)
        return (ex, ey)

    def along(self, axis, step):
        return self.at(step, 0, 0, 0) if axis == "x" else self.at(0, step, 0, 0)

    def greet(self):
        barrier = pltpu.get_barrier_semaphore()
        partners = [self.along(axis, s) for axis in ("x", "y") for s in (1, 2, 3)]
        partners += [self.at(0, 0, dz, dc) for dz, dc in NEAR[1:]]
        partners += [self.at(0, 0, 2, 0)]
        partners += [self.at(0, dy, 0, 1) for dy in (1, 2, 3)]
        for partner in partners:
            pl.semaphore_signal(barrier, inc=1, device_id=partner, device_id_type=MESH)
        pl.semaphore_wait(barrier, len(partners))


def remote(src, dst, send, recv, partner):
    return pltpu.make_async_remote_copy(
        src_ref=src, dst_ref=dst, send_sem=send, recv_sem=recv, device_id=partner, device_id_type=MESH
    )


def chunk(c):
    return pl.ds(pl.multiple_of(c * W, W), W)


def line(ref, c, axis, index, part=slice(0, 4)):
    if axis == "y":
        return ref.at[c, index, part]
    return ref.at[c, part, index]


def dispatch_kernel(
    pairs,
    tok, ids, weight, w_gate, w_up, s_gate, s_up,
    h_out, hs_out, comb, comb_far,
    ag, far, snd, rcv, snd_far, rcv_far, acc_g, acc_u, gate_v, up_v, sgu,
    meta, metas, metas_far, place_t, place_far, acc_s,
    load_sem, m_send, m_recv, p1_send, p1_recv, p2_send, p2_recv, fw_send, fw_recv,
    a_send, a_recv, f_send, f_recv, z_send, z_recv, y_send, y_recv,
):
    here = Place()
    x, y, z, core = here.x, here.y, here.z, here.c

    def load(i, which):
        rows = pl.ds(pl.multiple_of(i * 2 * W, 2 * W), 2 * W)
        src, dst = (
            (w_gate.at[0, rows], gate_v.at[i]),
            (w_up.at[0, rows], up_v.at[i]),
            (s_gate.at[rows], sgu.at[i, :, pl.ds(0, 128)]),
            (s_up.at[rows], sgu.at[i, :, pl.ds(128, 128)]),
        )[which]
        return pltpu.make_async_copy(src, dst, load_sem.at[which, i])

    def start_loads(i, carry):
        for which in range(4):
            load(i, which).start()
        return carry

    lane = lax.broadcasted_iota(jnp.int32, (64, 128), 1)
    hits = [ids[:, k : k + 1] == lane for k in range(8)]
    named = sum(jnp.where(hit, 1.0, 0.0) for hit in hits)
    lower = lax.broadcasted_iota(jnp.int32, (64, 64), 0) > lax.broadcasted_iota(jnp.int32, (64, 64), 1)
    before = dot(jnp.where(lower, 1.0, 0.0).astype(BF16), named.astype(BF16))
    info = jnp.zeros((64, 128), F32)
    for k in range(8):
        rank = jnp.sum(jnp.where(hits[k], before, 0.0), axis=1, keepdims=True)
        code = ids[:, k : k + 1].astype(F32) * 32.0 + rank
        info = jnp.where(lane == k, code, info)
        info = jnp.where(lane == 8 + k, weight[:, k : k + 1].astype(F32), info)
    meta[...] = info
    metas[y, x] = info

    def own(c, carry):
        ag[c, y, x] = tok[:, chunk(c)]
        return carry

    lax.fori_loop(0, 2 * pairs, own, 0)

    here.greet()

    def lead(half):
        return ("x", "y") if half == 0 else ("y", "x")

    def place(axis):
        return x if axis == "x" else y

    def first(c, half, s):
        partner = here.along(lead(half)[0], s)
        return remote(tok.at[:, chunk(c)], ag.at[c, y, x], p1_send.at[c, s - 1], p1_recv.at[c, s - 1], partner)

    def second(c, half, d):
        axis = lead(half)[1]
        block = line(ag, c, axis, place(axis))
        return remote(block, block, p2_send.at[c, d], p2_recv.at[c, d], here.along(axis, 1 + 2 * d))

    def onward(c, half, d):
        axis = lead(half)[1]
        origin = lax.rem(place(axis) + 3 - 2 * d, 4)
        block = line(ag, c, axis, origin, pl.ds(2 * d, 2))
        return remote(block, block, fw_send.at[c, d], fw_recv.at[c, d], here.along(axis, 1 + 2 * d))

    def opposite(c):
        return remote(tok.at[:, chunk(c)], far.at[c, x], a_send.at[c], a_recv.at[c], here.at(0, 0, 2, 0))

    def spread(c, s):
        return remote(far.at[c, x], far.at[c, x], f_send.at[c, s - 1], f_recv.at[c, s - 1], here.along("x", s))

    def near(c, b):
        dz, dc = NEAR[b]
        return remote(snd.at[c, b - 1], rcv.at[c, b], z_send.at[c, b - 1], z_recv.at[c, b - 1], here.at(0, 0, dz, dc))

    def near_far(c, j):
        dy, dc = FAR[j]
        return remote(
            snd_far.at[c, j - 1], rcv_far.at[c, j], y_send.at[c, j - 1], y_recv.at[c, j - 1], here.at(0, dy, 0, dc)
        )

    def meta_copy(stage, s):
        sems = m_send.at[stage, s - 1], m_recv.at[stage, s - 1]
        if stage == 0:
            return remote(meta, metas.at[y, x], *sems, here.along("x", s))
        if stage == 1:
            return remote(metas.at[y], metas.at[y], *sems, here.along("y", s))
        if stage == 2:
            return remote(meta, metas_far.at[x], *sems, here.at(0, 0, 2, 0))
        return remote(metas_far.at[x], metas_far.at[x], *sems, here.along("x", s))

    def start_first(i):
        for half in (0, 1):
            c = 2 * i + half
            for s in (2, 1, 3):
                first(c, half, s).start()
            opposite(c).start()

    def start_second(i):
        for half in (0, 1):
            c = 2 * i + half
            for s in (1, 2, 3):
                first(c, half, s).wait_recv()
            for d in (0, 1):
                second(c, half, d).start()
            opposite(c).wait_recv()
            for s in (2, 1, 3):
                spread(c, s).start()

    def start_onward(i):
        for half in (0, 1):
            c = 2 * i + half
            for d in (0, 1):
                second(c, half, d).wait_recv()
                onward(c, half, d).start()

    meta_copy(2, 1).start()
    for s in (2, 1, 3):
        meta_copy(0, s).start()
    start_first(0)
    start_first(1)
    for s in (1, 2, 3):
        meta_copy(0, s).wait_recv()
    for s in (2, 1, 3):
        meta_copy(1, s).start()
    meta_copy(2, 1).wait_recv()
    for s in (2, 1, 3):
        meta_copy(3, s).start()
    start_second(0)
    start_first(2)
    lax.fori_loop(0, pairs, start_loads, 0)

    def clear(r, carry):
        rows = pl.ds(pl.multiple_of(r * 64, 64), 64)
        acc_g[rows] = jnp.zeros((64, 1024), F32)
        acc_u[rows] = jnp.zeros((64, 1024), F32)
        acc_s[rows] = jnp.zeros((64, 256), F32)
        return carry

    start_second(1)
    start_onward(0)
    lax.fori_loop(0, 16, clear, 0)

    slot = lax.broadcasted_iota(jnp.int32, (8, 256), 1)[:1]
    group = lax.shift_right_logical(slot, 5)
    inner = lax.bitwise_and(slot, 7) + lax.bitwise_and(lax.shift_right_logical(slot, 3), 3) * 8192
    other = lax.bitwise_and(group + core, 1)
    outer = lax.shift_right_logical(group, 1)
    plane = lax.bitwise_and(z + outer + jnp.where(outer == 2, 1, 0), 3)
    want = jnp.where(outer == 3, -1, (here.ex * 8 + plane * 2 + other) * 32 + inner).astype(F32)
    row = lax.bitwise_and(y + outer, 3)
    want_far = ((row * 32 + x * 8 + z * 2 + other) * 32 + inner).astype(F32)
    source = lax.shift_right_logical(lax.broadcasted_iota(jnp.int32, (256, 128), 0), 6)[:, :1]
    shift = (source * 8192).astype(F32)

    def matrix(known, wanted):
        total = jnp.zeros((256, 256), F32)
        for k in range(8):
            hit = (known[:, k : k + 1] + shift) == wanted
            total = jnp.where(hit, known[:, 8 + k : 9 + k], total)
        return total.astype(BF16), jnp.where(total > 0.0, 1.0, 0.0).T.astype(BF16)

    for s in (1, 2, 3):
        meta_copy(1, s).wait_recv()

    def matrices(q, carry):
        comb[q], place_t[q] = matrix(metas[q].reshape(256, 128), want)
        return carry

    lax.fori_loop(0, 4, matrices, 0)
    for s in (1, 2, 3):
        meta_copy(3, s).wait_recv()
    comb_far[...], place_far[...] = matrix(metas_far[...].reshape(256, 128), want_far)

    def compact(i):
        for half in (0, 1):
            c = 2 * i + half
            for d in (0, 1):
                onward(c, half, d).wait_recv()

            for q in range(4):
                rows = dot(place_t[q, :192], ag[c, q].reshape(256, W)).astype(BF16).reshape(6, 32, W)
                span = slice(q * 32, q * 32 + 32)
                rcv[c, 0, span] = rows[0]
                snd[c, :, span] = rows[1:]
            for b in range(1, 6):
                near(c, b).start()
            for s in (1, 2, 3):
                spread(c, s).wait_recv()
            rows = dot(place_far[...], far[c].reshape(256, W)).astype(BF16).reshape(8, 32, W)
            rcv_far[c, 0] = rows[0]
            snd_far[c] = rows[1:]
            for j in (4, 5, 2, 3, 6, 7, 1):
                near_far(c, j).start()

    def shared(i):
        for which in (2, 3):
            load(i, which).wait()

        both = jnp.concatenate([ag[2 * i].reshape(1024, W), ag[2 * i + 1].reshape(1024, W)], axis=1)
        acc_s[...] += dot(both, sgu[i])

    def expert(i):
        for which in (0, 1):
            load(i, which).wait()
        for half in (0, 1):
            c = 2 * i + half
            for b in range(1, 6):
                near(c, b).wait_recv()
            for j in range(1, 8):
                near_far(c, j).wait_recv()

        def add(rows, left, right):
            both = jnp.concatenate([left, right], axis=1)
            acc_g[rows] += dot(both, gate_v[i])
            acc_u[rows] += dot(both, up_v[i])

        def tile(m, carry):
            blocks = pl.ds(2 * m, 2)
            add(
                pl.ds(pl.multiple_of(m * 256, 256), 256),
                rcv[2 * i, blocks].reshape(256, W),
                rcv[2 * i + 1, blocks].reshape(256, W),
            )
            return carry

        lax.fori_loop(0, 3, tile, 0)
        add(pl.ds(768, 256), rcv_far[2 * i].reshape(256, W), rcv_far[2 * i + 1].reshape(256, W))

    def step(i, carry):
        @pl.when(i + 3 < pairs)
        def _():
            start_first(i + 3)

        @pl.when(i + 2 < pairs)
        def _():
            start_second(i + 2)

        @pl.when(i + 1 < pairs)
        def _():
            start_onward(i + 1)

        @pl.when(i < pairs)
        def _():
            compact(i)
            shared(i)

        @pl.when(i >= LAG)
        def _():
            expert(i - LAG)

        return carry

    lax.fori_loop(0, pairs + LAG, step, 0)

    def finish(r, carry):
        rows = pl.ds(pl.multiple_of(r * 64, 64), 64)
        h_out[rows] = (jax.nn.silu(acc_g[rows]) * acc_u[rows]).astype(BF16)
        both = acc_s[rows]
        hs_out[rows] = (jax.nn.silu(both[:, :128]) * both[:, 128:]).astype(BF16)
        return carry

    lax.fori_loop(0, 16, finish, 0)

    for stage in (0, 1, 3):
        for s in (1, 2, 3):
            meta_copy(stage, s).wait_send()
    meta_copy(2, 1).wait_send()

    def drain(i, carry):
        for half in (0, 1):
            c = 2 * i + half
            for s in (1, 2, 3):
                first(c, half, s).wait_send()
                spread(c, s).wait_send()
            opposite(c).wait_send()
            for d in (0, 1):
                second(c, half, d).wait_send()
                onward(c, half, d).wait_send()
            for b in range(1, 6):
                near(c, b).wait_send()
            for j in range(1, 8):
                near_far(c, j).wait_send()
        return carry

    lax.fori_loop(0, pairs, drain, 0)


def return_kernel(
    pairs,
    h, hs, comb, comb_far, w_down, s_down,
    out,
    down_v, sd_v, snd, rcv, snd_far, rcv_far, part, relay, got1, half_sum, got2, part_far, got_far, sum_far, got_home,
    load_sem, z_send, z_recv, y_send, y_recv, r0_send, r0_recv, r1_send, r1_recv, r2_send, r2_recv,
    f_send, f_recv, a_send, a_recv,
):
    here = Place()
    x, y = here.x, here.y

    def load(i, which):
        columns = pl.ds(pl.multiple_of(i * 2 * W, 2 * W), 2 * W)
        src, dst = (
            (w_down.at[0, :, columns], down_v.at[i]),
            (s_down.at[:, columns], sd_v.at[i]),
        )[which]
        return pltpu.make_async_copy(src, dst, load_sem.at[which, i])

    def start_loads(i, carry):
        for which in (0, 1):
            load(i, which).start()
        return carry

    lax.fori_loop(0, pairs, start_loads, 0)
    here.greet()

    def lead(half):
        return ("y", "x") if half == 0 else ("x", "y")

    def place(axis, step=0):
        return lax.rem((x if axis == "x" else y) + step, 4)

    def near(c, b):
        dz, dc = NEAR[b]
        return remote(
            snd.at[c, b - 1], rcv.at[c, b], z_send.at[c, b - 1], z_recv.at[c, b - 1], here.at(0, 0, 4 - dz, dc)
        )

    def near_far(c, j):
        dy, dc = FAR[j]
        return remote(
            snd_far.at[c, j - 1], rcv_far.at[c, j], y_send.at[c, j - 1], y_recv.at[c, j - 1], here.at(0, 4 - dy, 0, dc)
        )

    def through(c, half, d):
        axis = lead(half)[0]
        block = line(part, c, axis, place(axis, 2), pl.ds(2 * d, 2))
        return remote(block, relay.at[c, d], r0_send.at[c, d], r0_recv.at[c, d], here.along(axis, 3 - 2 * d))

    def first(c, half, d):
        axis = lead(half)[0]
        block = line(part, c, axis, place(axis, 3 - 2 * d))
        return remote(block, got1.at[c, d], r1_send.at[c, d], r1_recv.at[c, d], here.along(axis, 3 - 2 * d))

    def second(c, half, s):
        axis = lead(half)[1]
        block = half_sum.at[c, place(axis, s)]
        return remote(block, got2.at[c, s - 1], r2_send.at[c, s - 1], r2_recv.at[c, s - 1], here.along(axis, s))

    def gather_far(c, s):
        block = part_far.at[c, place("x", s)]
        return remote(block, got_far.at[c, s - 1], f_send.at[c, s - 1], f_recv.at[c, s - 1], here.along("x", s))

    def home(c):
        return remote(sum_far.at[c], got_home.at[c], a_send.at[c], a_recv.at[c], here.at(0, 0, 2, 0))

    def down(i):
        load(i, 0).wait()
        for m in range(4):
            result = dot(h[m * 256 : m * 256 + 256], down_v[i]).astype(BF16)
            for half in (0, 1):
                c = 2 * i + half
                piece = result[:, half * W : half * W + W]
                if m == 3:
                    piece = piece.reshape(8, 32, W)
                    rcv_far[c, 0] = piece[0]
                    snd_far[c] = piece[1:]
                elif m == 0:
                    rcv[c, 0] = piece[:128]
                    snd[c, 0] = piece[128:]
                else:
                    snd[c, 2 * m - 1] = piece[:128]
                    snd[c, 2 * m] = piece[128:]
        for half in (0, 1):
            c = 2 * i + half
            for b in range(1, 6):
                near(c, b).start()
            for j in (4, 5, 2, 3, 6, 7, 1):
                near_far(c, j).start()

    def combine(i):
        load(i, 1).wait()
        for half in (0, 1):
            c = 2 * i + half
            for j in range(1, 8):
                near_far(c, j).wait_recv()
            total = dot(comb_far[...], rcv_far[c].reshape(256, W))
            part_far[c] = total.astype(BF16).reshape(4, 64, W)
            for b in range(1, 6):
                near(c, b).wait_recv()

            for q in range(4):
                rows = rcv[c, :, q * 32 : q * 32 + 32].reshape(192, W)
                rows = jnp.concatenate([sd_v[i, :, half * W : half * W + W], rows], axis=0)
                total = dot(jnp.concatenate([hs[q * 256 : q * 256 + 256], comb[q, :, :192]], axis=1), rows)
                part[c, q] = total.astype(BF16).reshape(4, 64, W)
            for d in (0, 1):
                through(c, half, d).start()
            for s in (2, 1, 3):
                gather_far(c, s).start()

    def pass_on(i):
        for half in (0, 1):
            c = 2 * i + half
            axis = lead(half)[0]
            for d in (0, 1):
                through(c, half, d).wait_recv()
                target = place(axis, 3 - 2 * d)
                for b in (2 * d, 2 * d + 1):
                    where = (c, target, b) if axis == "y" else (c, b, target)
                    part[where] = (part[where].astype(F32) + relay[c, d, b - 2 * d].astype(F32)).astype(BF16)
            for d in (0, 1):
                first(c, half, d).start()
            total = jnp.zeros((64, W), F32)
            for s in (1, 2, 3):
                gather_far(c, s).wait_recv()
                total += got_far[c, s - 1].astype(F32)
            sum_far[c] = (total + part_far[c, x].astype(F32)).astype(BF16)
            home(c).start()

    def reduce(i):
        for half in (0, 1):
            c = 2 * i + half
            for d in (0, 1):
                first(c, half, d).wait_recv()
            for b in range(4):
                mine = part[c, y, b] if half == 0 else part[c, b, x]
                total = mine.astype(F32) + got1[c, 0, b].astype(F32) + got1[c, 1, b].astype(F32)
                half_sum[c, b] = total.astype(BF16)
            for s in (2, 1, 3):
                second(c, half, s).start()

    def final(i):
        for half in (0, 1):
            c = 2 * i + half
            home(c).wait_recv()
            total = got_home[c].astype(F32) + half_sum[c, place(lead(half)[1])].astype(F32)
            for s in (1, 2, 3):
                second(c, half, s).wait_recv()
                total += got2[c, s - 1].astype(F32)
            out[:, chunk(c)] = total.astype(BF16)

    def step(i, carry):
        @pl.when(i < pairs)
        def _():
            down(i)

        @pl.when((i >= 2) & (i < pairs + 2))
        def _():
            pass_on(i - 2)

        @pl.when((i >= 3) & (i < pairs + 3))
        def _():
            reduce(i - 3)

        @pl.when(i >= 4)
        def _():
            final(i - 4)

        @pl.when((i >= 1) & (i < pairs + 1))
        def _():
            combine(i - 1)

        return carry

    lax.fori_loop(0, pairs + 4, step, 0)

    def drain(i, carry):
        for half in (0, 1):
            c = 2 * i + half
            for d in (0, 1):
                through(c, half, d).wait_send()
                first(c, half, d).wait_send()
            for s in (1, 2, 3):
                second(c, half, s).wait_send()
                gather_far(c, s).wait_send()
            home(c).wait_send()
            for b in range(1, 6):
                near(c, b).wait_send()
            for j in range(1, 8):
                near_far(c, j).wait_send()
        return carry

    lax.fori_loop(0, pairs, drain, 0)


def shards(
    tokens, route_ids, route_weight, w_gate, w_up, w_down, shared_gate, shared_up, shared_down
):
    width = tokens.shape[1]
    pairs = width // (2 * W)
    n = 2 * pairs
    vmem = pl.BlockSpec(memory_space=pltpu.VMEM)
    hbm = pl.BlockSpec(memory_space=pl.ANY)

    def both(*shape):
        return [pltpu.SemaphoreType.DMA(shape)] * 2

    def held(*shape, dtype=BF16):
        return pltpu.VMEM(shape, dtype)

    hidden, shared_hidden, comb, comb_far = pl.pallas_call(
        functools.partial(dispatch_kernel, pairs),
        out_shape=(
            jax.ShapeDtypeStruct((1024, 1024), BF16),
            jax.ShapeDtypeStruct((1024, 128), BF16),
            jax.ShapeDtypeStruct((4, 256, 256), BF16),
            jax.ShapeDtypeStruct((256, 256), BF16),
        ),
        in_specs=[vmem] * 3 + [hbm] * 4,
        out_specs=(vmem,) * 4,
        scratch_shapes=[
            held(n, 4, 4, 64, W),
            held(n, 4, 64, W),
            held(n, 5, 128, W),
            held(n, 6, 128, W),
            held(n, 7, 32, W),
            held(n, 8, 32, W),
            held(1024, 1024, dtype=F32),
            held(1024, 1024, dtype=F32),
            held(pairs, 2 * W, 1024),
            held(pairs, 2 * W, 1024),
            held(pairs, 2 * W, 256),
            held(64, 128, dtype=F32),
            held(4, 4, 64, 128, dtype=F32),
            held(4, 64, 128, dtype=F32),
            held(4, 256, 256),
            held(256, 256),
            held(1024, 256, dtype=F32),
            pltpu.SemaphoreType.DMA((4, pairs)),
            *both(4, 3), *both(n, 3), *both(n, 2), *both(n, 2),
            *both(n), *both(n, 3), *both(n, 5), *both(n, 7),
        ],
        compiler_params=pltpu.CompilerParams(
            collective_id=0, has_side_effects=True, vmem_limit_bytes=60 * 2**20
        ),
        name="dispatch",
    )(tokens, route_ids, route_weight, w_gate, w_up, shared_gate, shared_up)
    return pl.pallas_call(
        functools.partial(return_kernel, pairs),
        out_shape=jax.ShapeDtypeStruct((64, width), BF16),
        in_specs=[vmem] * 4 + [hbm] * 2,
        out_specs=vmem,
        scratch_shapes=[
            held(pairs, 1024, 2 * W),
            held(pairs, 128, 2 * W),
            held(n, 5, 128, W),
            held(n, 6, 128, W),
            held(n, 7, 32, W),
            held(n, 8, 32, W),
            held(n, 4, 4, 64, W),
            held(n, 2, 2, 64, W),
            held(n, 2, 4, 64, W),
            held(n, 4, 64, W),
            held(n, 3, 64, W),
            held(n, 4, 64, W),
            held(n, 3, 64, W),
            held(n, 64, W),
            held(n, 64, W),
            pltpu.SemaphoreType.DMA((2, pairs)),
            *both(n, 5), *both(n, 7), *both(n, 2), *both(n, 2), *both(n, 3), *both(n, 3), *both(n),
        ],
        compiler_params=pltpu.CompilerParams(
            collective_id=1, has_side_effects=True, vmem_limit_bytes=60 * 2**20
        ),
        name="bring_back",
    )(hidden, shared_hidden, comb, comb_far, w_down, shared_down)


def solution(mesh):
    in_specs = (
        P(("ex", "ey"), None),
        P(("ex", "ey"), None),
        P(("ex", "ey"), None),
        P(("ex", "ey"), None, None),
        P(("ex", "ey"), None, None),
        P(("ex", "ey"), None, None),
        P(None, "ex"),
        P(None, "ex"),
        P("ex", None),
    )
    out_specs = P(("ex", "ey"), None)
    return jax.shard_map(shards, mesh=mesh, in_specs=in_specs, out_specs=out_specs, check_vma=False)
```

time: 225 us -> 196 us (0.87); the launches traced: 225 us -> 193 us
  Pallas kernels: 220 us -> 189 us
    pallas_call x1, Pallas kernels: 117 us -> 97 us  [shards(): pl.pallas_call(functools.partial(dispatch_kernel, pairs), out_shape=(jax....]
    pallas_call x1, Pallas kernels: 103 us -> 91.6 us  [shards(): pl.pallas_call(functools.partial(return_kernel, pairs), out_shape=jax.Sha...]
where the time goes in v2:
time: 196 us; the launch traced here: 193 us
  Pallas kernels  189 us (96%)
  local copies, waits for them, and re-layouts  4.56 us (2%)
    pallas_call x1, Pallas kernels, shards(): pl.pallas_call(functools.partial(dispatch_kernel, pairs), out_shape=(jax....  97 us
    pallas_call x1, Pallas kernels, shards(): pl.pallas_call(functools.partial(return_kernel, pairs), out_shape=jax.Sha...  91.6 us
    unnamed x3, local copies, waits for them, and re-layouts  4.56 us

profile of v2, /device:TPU:1, one launch (start us, length us, event | category | flops | bytes accessed | tf_op | source)
XLA Modules:
  0.0 193.2 jit_solution(17015892313332535506)
XLA Ops:
  0.0 1.4 copy.11.weight
  1.4 1.4 copy.10.ids
  2.7 97.0 %dispatch.1 = (bf16[1024,1024]{1,0:T(8,128)(2,1)}, bf16[1024,128]{1,0:T(8,128)(2,1)}, bf16[4,256,256]{2,1,0:T(8,128)(2,1)}, bf16[256,256]{1,0:T(8,128)(2,1)}) custom-call(bf16[64,3584]{1,0:T(8,128)(2,1)} %tok.1, s32[64,8]{1,0:T(8,128)} %copy.10.ids, bf16[64,8]{1,0:T(8,128)(2,1)} %copy.11.weight, bf16[1,3584,1024]{2,1,0:T(8,128)(2,1)} %w_gate.1, ...), custom_call_target="tpu_custom_call" | custom-call | tf_op jit(solution)/shard_map/dispatch/pallas_call | solution.py:574
  99.8 91.6 %bring_back.1 = bf16[64,3584]{1,0:T(8,128)(2,1)} custom-call(bf16[1024,1024]{1,0:T(8,128)(2,1)} %get-tuple-element.9.h, bf16[1024,128]{1,0:T(8,128)(2,1)} %get-tuple-element.10.hs, bf16[4,256,256]{2,1,0:T(8,128)(2,1)} %get-tuple-element.11.comb, bf16[256,256]{1,0:T(8,128)(2,1)} %get-tuple-element.12.comb_far, bf16[1,1024,3584]{2,1,0:T(8,128)(2,1)} %w_down.1, ...), custom_call_target="tpu_custom_call" | custom-call | tf_op jit(solution)/shard_map/bring_back/pallas_call | solution.py:611
  191.4 1.8 copy.13

commit v3 on v2

--- a/solution.py
+++ b/solution.py
@@ -10,7 +10,10 @@
 MESH = pl.DeviceIdType.MESH
 F32 = jnp.float32
 BF16 = jnp.bfloat16
-LAG = 2
+LAG = 1
+FIRST, SECOND, ONWARD = 3, 2, 1
+COMBINE, PASS, REDUCE, FINAL = 2, 5, 8, 11
+STRAIGHT_BACK = 0
 W = 256
 
 
@@ -48,6 +51,14 @@
         for partner in partners:
             pl.semaphore_signal(barrier, inc=1, device_id=partner, device_id_type=MESH)
         pl.semaphore_wait(barrier, len(partners))
+
+
+def when(condition, action):
+    if isinstance(condition, bool):
+        if condition:
+            action()
+    else:
+        pl.when(condition)(action)
 
 
 def remote(src, dst, send, recv, partner):
@@ -93,26 +104,6 @@
             load(i, which).start()
         return carry
 
-    lane = lax.broadcasted_iota(jnp.int32, (64, 128), 1)
-    hits = [ids[:, k : k + 1] == lane for k in range(8)]
-    named = sum(jnp.where(hit, 1.0, 0.0) for hit in hits)
-    lower = lax.broadcasted_iota(jnp.int32, (64, 64), 0) > lax.broadcasted_iota(jnp.int32, (64, 64), 1)
-    before = dot(jnp.where(lower, 1.0, 0.0).astype(BF16), named.astype(BF16))
-    info = jnp.zeros((64, 128), F32)
-    for k in range(8):
-        rank = jnp.sum(jnp.where(hits[k], before, 0.0), axis=1, keepdims=True)
-        code = ids[:, k : k + 1].astype(F32) * 32.0 + rank
-        info = jnp.where(lane == k, code, info)
-        info = jnp.where(lane == 8 + k, weight[:, k : k + 1].astype(F32), info)
-    meta[...] = info
-    metas[y, x] = info
-
-    def own(c, carry):
-        ag[c, y, x] = tok[:, chunk(c)]
-        return carry
-
-    lax.fori_loop(0, 2 * pairs, own, 0)
-
     here.greet()
 
     def lead(half):
@@ -187,21 +178,27 @@
                 second(c, half, d).wait_recv()
                 onward(c, half, d).start()
 
-    meta_copy(2, 1).start()
-    for s in (2, 1, 3):
-        meta_copy(0, s).start()
-    start_first(0)
-    start_first(1)
-    for s in (1, 2, 3):
-        meta_copy(0, s).wait_recv()
-    for s in (2, 1, 3):
-        meta_copy(1, s).start()
-    meta_copy(2, 1).wait_recv()
-    for s in (2, 1, 3):
-        meta_copy(3, s).start()
-    start_second(0)
-    start_first(2)
-    lax.fori_loop(0, pairs, start_loads, 0)
+    def meta_of_slots():
+        pad = jnp.zeros((64, 128), F32)
+        turned_ids = jnp.concatenate([ids[...].astype(F32), jnp.zeros((120, 64), F32)], axis=0).T
+        turned_weight = jnp.concatenate([weight[...].astype(F32), jnp.zeros((120, 64), F32)], axis=0).T
+        lane = lax.broadcasted_iota(jnp.int32, (64, 128), 1)
+        name = lane.astype(F32)
+        hits = [turned_ids[:, k : k + 1] == name for k in range(8)]
+        named = sum(jnp.where(hit, 1.0, 0.0) for hit in hits)
+        lower = lax.broadcasted_iota(jnp.int32, (64, 64), 0) > lax.broadcasted_iota(jnp.int32, (64, 64), 1)
+        before = dot(jnp.where(lower, 1.0, 0.0).astype(BF16), named.astype(BF16))
+        info = pad
+        for k in range(8):
+            rank = jnp.sum(jnp.where(hits[k], before, 0.0), axis=1, keepdims=True)
+            info = jnp.where(lane == k, turned_ids[:, k : k + 1] * 32.0 + rank, info)
+            info = jnp.where(lane == 8 + k, turned_weight[:, k : k + 1], info)
+        meta[...] = info
+        metas[y, x] = info
+
+    def own(c, carry):
+        ag[c, y, x] = tok[:, chunk(c)]
+        return carry
 
     def clear(r, carry):
         rows = pl.ds(pl.multiple_of(r * 64, 64), 64)
@@ -210,9 +207,32 @@
         acc_s[rows] = jnp.zeros((64, 256), F32)
         return carry
 
-    start_second(1)
-    start_onward(0)
+    start_first(0)
+    lax.fori_loop(0, 2 * pairs, own, 0)
+    meta_of_slots()
+    meta_copy(2, 1).start()
+    for s in (2, 1, 3):
+        meta_copy(0, s).start()
+    for i in range(1, FIRST):
+        start_first(i)
+        if i == 1:
+            start_second(0)
+        if i == 2:
+            for s in (1, 2, 3):
+                meta_copy(0, s).wait_recv()
+            for s in (2, 1, 3):
+                meta_copy(1, s).start()
+            meta_copy(2, 1).wait_recv()
+            for s in (2, 1, 3):
+                meta_copy(3, s).start()
+            lax.fori_loop(0, pairs, start_loads, 0)
     lax.fori_loop(0, 16, clear, 0)
+    for i in range(1, SECOND):
+        start_second(i)
+        if i == 1:
+            start_onward(0)
+    for i in range(1, ONWARD):
+        start_onward(i)
 
     slot = lax.broadcasted_iota(jnp.int32, (8, 256), 1)[:1]
     group = lax.shift_right_logical(slot, 5)
@@ -301,17 +321,17 @@
         add(pl.ds(768, 256), rcv_far[2 * i].reshape(256, W), rcv_far[2 * i + 1].reshape(256, W))
 
     def step(i, carry):
-        @pl.when(i + 3 < pairs)
+        @pl.when(i + FIRST < pairs)
         def _():
-            start_first(i + 3)
-
-        @pl.when(i + 2 < pairs)
+            start_first(i + FIRST)
+
+        @pl.when(i + SECOND < pairs)
         def _():
-            start_second(i + 2)
-
-        @pl.when(i + 1 < pairs)
+            start_second(i + SECOND)
+
+        @pl.when(i + ONWARD < pairs)
         def _():
-            start_onward(i + 1)
+            start_onward(i + ONWARD)
 
         @pl.when(i < pairs)
         def _():
@@ -363,12 +383,13 @@
     pairs,
     h, hs, comb, comb_far, w_down, s_down,
     out,
-    down_v, sd_v, snd, rcv, snd_far, rcv_far, part, relay, got1, half_sum, got2, part_far, got_far, sum_far, got_home,
+    down_v, sd_v, snd, rcv, rcv_two, snd_far, rcv_far, part, relay, got1, half_sum, got2, part_far, relay_far, got_far, sum_far, got_home,
     load_sem, z_send, z_recv, y_send, y_recv, r0_send, r0_recv, r1_send, r1_recv, r2_send, r2_recv,
-    f_send, f_recv, a_send, a_recv,
+    f_send, f_recv, g_send, g_recv, a_send, a_recv,
 ):
     here = Place()
     x, y = here.x, here.y
+    n = 2 * pairs
 
     def load(i, which):
         columns = pl.ds(pl.multiple_of(i * 2 * W, 2 * W), 2 * W)
@@ -401,8 +422,27 @@
     def near_far(c, j):
         dy, dc = FAR[j]
         return remote(
-            snd_far.at[c, j - 1], rcv_far.at[c, j], y_send.at[c, j - 1], y_recv.at[c, j - 1], here.at(0, 4 - dy, 0, dc)
+            snd_far.at[c, j], rcv_far.at[c, j], y_send.at[c, j], y_recv.at[c, j], here.at(0, 4 - dy, 0, dc)
         )
+
+    def near_two(c, j):
+        dy, dc = FAR[j]
+        rows = pl.ds(pl.multiple_of(lax.rem(y + 4 - dy, 4) * 32, 32), 32)
+        return remote(
+            snd_far.at[c, j], rcv_two.at[c, dc, rows], y_send.at[c, j], y_recv.at[c, j], here.at(0, 0, 2, dc)
+        )
+
+    def far_rows(c, what):
+        def straight():
+            for j in range(8):
+                getattr(near_two(c, j), what)()
+
+        def around():
+            for j in (4, 5, 2, 3, 6, 7, 1):
+                getattr(near_far(c, j), what)()
+
+        when(c >= n - STRAIGHT_BACK, straight)
+        when(c < n - STRAIGHT_BACK, around)
 
     def through(c, half, d):
         axis = lead(half)[0]
@@ -419,123 +459,135 @@
         block = half_sum.at[c, place(axis, s)]
         return remote(block, got2.at[c, s - 1], r2_send.at[c, s - 1], r2_recv.at[c, s - 1], here.along(axis, s))
 
-    def gather_far(c, s):
-        block = part_far.at[c, place("x", s)]
-        return remote(block, got_far.at[c, s - 1], f_send.at[c, s - 1], f_recv.at[c, s - 1], here.along("x", s))
+    def through_far(c, d):
+        block = part_far.at[c, place("x", 2), pl.ds(32 * d, 32)]
+        return remote(block, relay_far.at[c, d], g_send.at[c, d], g_recv.at[c, d], here.along("x", 3 - 2 * d))
+
+    def gather_far(c, d):
+        block = part_far.at[c, place("x", 3 - 2 * d)]
+        return remote(block, got_far.at[c, d], f_send.at[c, d], f_recv.at[c, d], here.along("x", 3 - 2 * d))
 
     def home(c):
         return remote(sum_far.at[c], got_home.at[c], a_send.at[c], a_recv.at[c], here.at(0, 0, 2, 0))
 
-    def down(i):
-        load(i, 0).wait()
+    def down(c, half):
+        i = lax.div(c, 2)
+        if half == 0:
+            load(i, 0).wait()
         for m in range(4):
-            result = dot(h[m * 256 : m * 256 + 256], down_v[i]).astype(BF16)
-            for half in (0, 1):
-                c = 2 * i + half
-                piece = result[:, half * W : half * W + W]
-                if m == 3:
-                    piece = piece.reshape(8, 32, W)
-                    rcv_far[c, 0] = piece[0]
-                    snd_far[c] = piece[1:]
-                elif m == 0:
-                    rcv[c, 0] = piece[:128]
-                    snd[c, 0] = piece[128:]
-                else:
-                    snd[c, 2 * m - 1] = piece[:128]
-                    snd[c, 2 * m] = piece[128:]
+            piece = dot(h[m * 256 : m * 256 + 256], down_v[i, :, half * W : half * W + W]).astype(BF16)
+            if m == 3:
+                piece = piece.reshape(8, 32, W)
+                rcv_far[c, 0] = piece[0]
+                snd_far[c] = piece
+            elif m == 0:
+                rcv[c, 0] = piece[:128]
+                snd[c, 0] = piece[128:]
+            else:
+                snd[c, 2 * m - 1] = piece[:128]
+                snd[c, 2 * m] = piece[128:]
+        for b in range(1, 6):
+            near(c, b).start()
+        far_rows(c, "start")
+
+    def combine(c, half):
+        i = lax.div(c, 2)
+        if half == 0:
+            load(i, 1).wait()
+        far_rows(c, "wait_recv")
+
+        def far_part():
+            total = dot(comb_far[...], rcv_far[c].reshape(256, W))
+            part_far[c] = total.astype(BF16).reshape(4, 64, W)
+            for d in (0, 1):
+                through_far(c, d).start()
+
+        def near_part(count):
+            for q in range(4):
+                span = slice(q * 32, q * 32 + 32)
+                rows = [sd_v[i, :, half * W : half * W + W], rcv[c, :, span].reshape(192, W)]
+                if count == 8:
+                    rows.append(rcv_two[c, :, span].reshape(64, W))
+                left = jnp.concatenate([hs[q * 256 : q * 256 + 256], comb[q, :, : count * 32]], axis=1)
+                part[c, q] = dot(left, jnp.concatenate(rows, axis=0)).astype(BF16).reshape(4, 64, W)
+
+        when(c < n - STRAIGHT_BACK, far_part)
+        for b in range(1, 6):
+            near(c, b).wait_recv()
+        when(c < n - STRAIGHT_BACK, lambda: near_part(6))
+        when(c >= n - STRAIGHT_BACK, lambda: near_part(8))
+        for d in (0, 1):
+            through(c, half, d).start()
+
+    def pass_on(c, half):
+        axis = lead(half)[0]
+        for d in (0, 1):
+            through(c, half, d).wait_recv()
+            target = place(axis, 3 - 2 * d)
+            for b in (2 * d, 2 * d + 1):
+                where = (c, target, b) if axis == "y" else (c, b, target)
+                part[where] = (part[where].astype(F32) + relay[c, d, b - 2 * d].astype(F32)).astype(BF16)
+        for d in (0, 1):
+            first(c, half, d).start()
+
+        def go():
+            for d in (0, 1):
+                through_far(c, d).wait_recv()
+                where = (c, place("x", 3 - 2 * d), slice(32 * d, 32 * d + 32))
+                part_far[where] = (part_far[where].astype(F32) + relay_far[c, d].astype(F32)).astype(BF16)
+            for d in (0, 1):
+                gather_far(c, d).start()
+
+        when(c < n - STRAIGHT_BACK, go)
+
+    def reduce(c, half):
+        for d in (0, 1):
+            first(c, half, d).wait_recv()
+        for b in range(4):
+            mine = part[c, y, b] if half == 0 else part[c, b, x]
+            total = mine.astype(F32) + got1[c, 0, b].astype(F32) + got1[c, 1, b].astype(F32)
+            half_sum[c, b] = total.astype(BF16)
+        for s in (2, 1, 3):
+            second(c, half, s).start()
+
+        def send_home():
+            total = part_far[c, x].astype(F32)
+            for d in (0, 1):
+                gather_far(c, d).wait_recv()
+                total += got_far[c, d].astype(F32)
+            sum_far[c] = total.astype(BF16)
+            home(c).start()
+
+        when(c < n - STRAIGHT_BACK, send_home)
+
+    def final(c, half):
+        total = half_sum[c, place(lead(half)[1])].astype(F32)
+        for s in (1, 2, 3):
+            second(c, half, s).wait_recv()
+            total += got2[c, s - 1].astype(F32)
+
+        def with_far():
+            home(c).wait_recv()
+            out[:, chunk(c)] = (total + got_home[c].astype(F32)).astype(BF16)
+
+        def without():
+            out[:, chunk(c)] = total.astype(BF16)
+
+        when(c < n - STRAIGHT_BACK, with_far)
+        when(c >= n - STRAIGHT_BACK, without)
+
+    def step(i, carry):
         for half in (0, 1):
             c = 2 * i + half
-            for b in range(1, 6):
-                near(c, b).start()
-            for j in (4, 5, 2, 3, 6, 7, 1):
-                near_far(c, j).start()
-
-    def combine(i):
-        load(i, 1).wait()
-        for half in (0, 1):
-            c = 2 * i + half
-            for j in range(1, 8):
-                near_far(c, j).wait_recv()
-            total = dot(comb_far[...], rcv_far[c].reshape(256, W))
-            part_far[c] = total.astype(BF16).reshape(4, 64, W)
-            for b in range(1, 6):
-                near(c, b).wait_recv()
-
-            for q in range(4):
-                rows = rcv[c, :, q * 32 : q * 32 + 32].reshape(192, W)
-                rows = jnp.concatenate([sd_v[i, :, half * W : half * W + W], rows], axis=0)
-                total = dot(jnp.concatenate([hs[q * 256 : q * 256 + 256], comb[q, :, :192]], axis=1), rows)
-                part[c, q] = total.astype(BF16).reshape(4, 64, W)
-            for d in (0, 1):
-                through(c, half, d).start()
-            for s in (2, 1, 3):
-                gather_far(c, s).start()
-
-    def pass_on(i):
-        for half in (0, 1):
-            c = 2 * i + half
-            axis = lead(half)[0]
-            for d in (0, 1):
-                through(c, half, d).wait_recv()
-                target = place(axis, 3 - 2 * d)
-                for b in (2 * d, 2 * d + 1):
-                    where = (c, target, b) if axis == "y" else (c, b, target)
-                    part[where] = (part[where].astype(F32) + relay[c, d, b - 2 * d].astype(F32)).astype(BF16)
-            for d in (0, 1):
-                first(c, half, d).start()
-            total = jnp.zeros((64, W), F32)
-            for s in (1, 2, 3):
-                gather_far(c, s).wait_recv()
-                total += got_far[c, s - 1].astype(F32)
-            sum_far[c] = (total + part_far[c, x].astype(F32)).astype(BF16)
-            home(c).start()
-
-    def reduce(i):
-        for half in (0, 1):
-            c = 2 * i + half
-            for d in (0, 1):
-                first(c, half, d).wait_recv()
-            for b in range(4):
-                mine = part[c, y, b] if half == 0 else part[c, b, x]
-                total = mine.astype(F32) + got1[c, 0, b].astype(F32) + got1[c, 1, b].astype(F32)
-                half_sum[c, b] = total.astype(BF16)
-            for s in (2, 1, 3):
-                second(c, half, s).start()
-
-    def final(i):
-        for half in (0, 1):
-            c = 2 * i + half
-            home(c).wait_recv()
-            total = got_home[c].astype(F32) + half_sum[c, place(lead(half)[1])].astype(F32)
-            for s in (1, 2, 3):
-                second(c, half, s).wait_recv()
-                total += got2[c, s - 1].astype(F32)
-            out[:, chunk(c)] = total.astype(BF16)
-
-    def step(i, carry):
-        @pl.when(i < pairs)
-        def _():
-            down(i)
-
-        @pl.when((i >= 2) & (i < pairs + 2))
-        def _():
-            pass_on(i - 2)
-
-        @pl.when((i >= 3) & (i < pairs + 3))
-        def _():
-            reduce(i - 3)
-
-        @pl.when(i >= 4)
-        def _():
-            final(i - 4)
-
-        @pl.when((i >= 1) & (i < pairs + 1))
-        def _():
-            combine(i - 1)
-
-        return carry
-
-    lax.fori_loop(0, pairs + 4, step, 0)
+            for stage, lag in ((down, 0), (pass_on, PASS), (reduce, REDUCE), (final, FINAL), (combine, COMBINE)):
+
+                @pl.when((c >= lag) & (c < n + lag))
+                def _():
+                    stage(c - lag, (half + lag) % 2)
+
+        return carry
+
+    lax.fori_loop(0, pairs + (FINAL + 1) // 2, step, 0)
 
     def drain(i, carry):
         for half in (0, 1):
@@ -545,12 +597,17 @@
                 first(c, half, d).wait_send()
             for s in (1, 2, 3):
                 second(c, half, s).wait_send()
-                gather_far(c, s).wait_send()
-            home(c).wait_send()
+
+            def sent():
+                for d in (0, 1):
+                    through_far(c, d).wait_send()
+                    gather_far(c, d).wait_send()
+                home(c).wait_send()
+
+            when(c < n - STRAIGHT_BACK, sent)
             for b in range(1, 6):
                 near(c, b).wait_send()
-            for j in range(1, 8):
-                near_far(c, j).wait_send()
+            far_rows(c, "wait_send")
         return carry
 
     lax.fori_loop(0, pairs, drain, 0)
@@ -607,7 +664,7 @@
             collective_id=0, has_side_effects=True, vmem_limit_bytes=60 * 2**20
         ),
         name="dispatch",
-    )(tokens, route_ids, route_weight, w_gate, w_up, shared_gate, shared_up)
+    )(tokens, route_ids.T, route_weight.T, w_gate, w_up, shared_gate, shared_up)
     return pl.pallas_call(
         functools.partial(return_kernel, pairs),
         out_shape=jax.ShapeDtypeStruct((64, width), BF16),
@@ -618,7 +675,8 @@
             held(pairs, 128, 2 * W),
             held(n, 5, 128, W),
             held(n, 6, 128, W),
-            held(n, 7, 32, W),
+            held(n, 2, 128, W),
+            held(n, 8, 32, W),
             held(n, 8, 32, W),
             held(n, 4, 4, 64, W),
             held(n, 2, 2, 64, W),
@@ -626,11 +684,13 @@
             held(n, 4, 64, W),
             held(n, 3, 64, W),
             held(n, 4, 64, W),
-            held(n, 3, 64, W),
+            held(n, 2, 32, W),
+            held(n, 2, 64, W),
             held(n, 64, W),
             held(n, 64, W),
             pltpu.SemaphoreType.DMA((2, pairs)),
-            *both(n, 5), *both(n, 7), *both(n, 2), *both(n, 2), *both(n, 3), *both(n, 3), *both(n),
+            *both(n, 5), *both(n, 8), *both(n, 2), *both(n, 2), *both(n, 3),
+            *both(n, 2), *both(n, 2), *both(n),
         ],
         compiler_params=pltpu.CompilerParams(
             collective_id=1, has_side_effects=True, vmem_limit_bytes=60 * 2**20

time: 196 us -> 178 us (0.908); the launches traced: 193 us -> 178 us
  Pallas kernels: 189 us -> 176 us
  local copies, waits for them, and re-layouts: 4.56 us -> 1.82 us
    pallas_call x1, Pallas kernels: 91.6 us -> 80.4 us  [shards(): pl.pallas_call(functools.partial(return_kernel, pairs), out_shape=jax.Sha...]
    unnamed x3 -> x1, local copies, waits for them, and re-layouts: 4.56 us -> 1.82 us
where the time goes in v3:
time: 178 us
  Pallas kernels  176 us (99%)
  local copies, waits for them, and re-layouts  1.82 us (1%)
    pallas_call x1, Pallas kernels, shards(): pl.pallas_call(functools.partial(dispatch_kernel, pairs), out_shape=(jax....  95.5 us
    pallas_call x1, Pallas kernels, shards(): pl.pallas_call(functools.partial(return_kernel, pairs), out_shape=jax.Sha...  80.4 us

profile of v3, /device:TPU:1, one launch (start us, length us, event | category | flops | bytes accessed | tf_op | source)
XLA Modules:
  0.0 177.7 jit_solution(9239025776643558222)
XLA Ops:
  0.0 95.5 %dispatch.1 = (bf16[1024,1024]{1,0:T(8,128)(2,1)}, bf16[1024,128]{1,0:T(8,128)(2,1)}, bf16[4,256,256]{2,1,0:T(8,128)(2,1)}, bf16[256,256]{1,0:T(8,128)(2,1)}) custom-call(bf16[64,3584]{1,0:T(8,128)(2,1)} %tok.1, s32[8,64]{1,0:T(8,128)} %bitcast.2, bf16[8,64]{1,0:T(8,128)(2,1)} %bitcast.3, bf16[1,3584,1024]{2,1,0:T(8,128)(2,1)} %w_gate.1, ...), custom_call_target="tpu_custom_call" | custom-call | tf_op jit(solution)/shard_map/dispatch/pallas_call | solution.py:631
  95.5 80.4 %bring_back.1 = bf16[64,3584]{1,0:T(8,128)(2,1)} custom-call(bf16[1024,1024]{1,0:T(8,128)(2,1)} %get-tuple-element.9.h, bf16[1024,128]{1,0:T(8,128)(2,1)} %get-tuple-element.10.hs, bf16[4,256,256]{2,1,0:T(8,128)(2,1)} %get-tuple-element.11.comb, bf16[256,256]{1,0:T(8,128)(2,1)} %get-tuple-element.12.comb_far, bf16[1,1024,3584]{2,1,0:T(8,128)(2,1)} %w_down.1, ...), custom_call_target="tpu_custom_call" | custom-call | tf_op jit(solution)/shard_map/bring_back/pallas_call | solution.py:668
  175.9 1.8 %copy.11 = bf16[64,3584]{1,0:T(8,128)(2,1)} copy(bf16[64,3584]{1,0:T(8,128)(2,1)} %bring_back.1) | data formatting | bytes 917504

commit v4 on v3

--- a/solution.py
+++ b/solution.py
@@ -84,7 +84,7 @@
     ag, far, snd, rcv, snd_far, rcv_far, acc_g, acc_u, gate_v, up_v, sgu,
     meta, metas, metas_far, place_t, place_far, acc_s,
     load_sem, m_send, m_recv, p1_send, p1_recv, p2_send, p2_recv, fw_send, fw_recv,
-    a_send, a_recv, f_send, f_recv, z_send, z_recv, y_send, y_recv,
+    a_send, a_recv, f_send, f_recv, g_send, g_recv, z_send, z_recv, y_send, y_recv,
 ):
     here = Place()
     x, y, z, core = here.x, here.y, here.z, here.c
@@ -130,8 +130,12 @@
     def opposite(c):
         return remote(tok.at[:, chunk(c)], far.at[c, x], a_send.at[c], a_recv.at[c], here.at(0, 0, 2, 0))
 
-    def spread(c, s):
-        return remote(far.at[c, x], far.at[c, x], f_send.at[c, s - 1], f_recv.at[c, s - 1], here.along("x", s))
+    def spread(c, d):
+        return remote(far.at[c, x], far.at[c, x], f_send.at[c, d], f_recv.at[c, d], here.along("x", 1 + 2 * d))
+
+    def spread_on(c, d):
+        block = far.at[c, lax.rem(x + 3 - 2 * d, 4), pl.ds(32 * d, 32)]
+        return remote(block, block, g_send.at[c, d], g_recv.at[c, d], here.along("x", 1 + 2 * d))
 
     def near(c, b):
         dz, dc = NEAR[b]
@@ -158,7 +162,6 @@
             c = 2 * i + half
             for s in (2, 1, 3):
                 first(c, half, s).start()
-            opposite(c).start()
 
     def start_second(i):
         for half in (0, 1):
@@ -168,8 +171,8 @@
             for d in (0, 1):
                 second(c, half, d).start()
             opposite(c).wait_recv()
-            for s in (2, 1, 3):
-                spread(c, s).start()
+            for d in (0, 1):
+                spread(c, d).start()
 
     def start_onward(i):
         for half in (0, 1):
@@ -177,6 +180,9 @@
             for d in (0, 1):
                 second(c, half, d).wait_recv()
                 onward(c, half, d).start()
+            for d in (0, 1):
+                spread(c, d).wait_recv()
+                spread_on(c, d).start()
 
     def meta_of_slots():
         pad = jnp.zeros((64, 128), F32)
@@ -207,7 +213,12 @@
         acc_s[rows] = jnp.zeros((64, 256), F32)
         return carry
 
+    def start_opposite(c, carry):
+        opposite(c).start()
+        return carry
+
     start_first(0)
+    lax.fori_loop(0, 2 * pairs, start_opposite, 0)
     lax.fori_loop(0, 2 * pairs, own, 0)
     meta_of_slots()
     meta_copy(2, 1).start()
@@ -278,8 +289,8 @@
                 snd[c, :, span] = rows[1:]
             for b in range(1, 6):
                 near(c, b).start()
-            for s in (1, 2, 3):
-                spread(c, s).wait_recv()
+            for d in (0, 1):
+                spread_on(c, d).wait_recv()
             rows = dot(place_far[...], far[c].reshape(256, W)).astype(BF16).reshape(8, 32, W)
             rcv_far[c, 0] = rows[0]
             snd_far[c] = rows[1:]
@@ -365,9 +376,10 @@
             c = 2 * i + half
             for s in (1, 2, 3):
                 first(c, half, s).wait_send()
-                spread(c, s).wait_send()
             opposite(c).wait_send()
             for d in (0, 1):
+                spread(c, d).wait_send()
+                spread_on(c, d).wait_send()
                 second(c, half, d).wait_send()
                 onward(c, half, d).wait_send()
             for b in range(1, 6):
@@ -381,8 +393,9 @@
 
 def return_kernel(
     pairs,
-    h, hs, comb, comb_far, w_down, s_down,
+    h_in, hs_in, comb_in, comb_far_in, w_down, s_down,
     out,
+    h, hs, comb, comb_far, in_sem,
     down_v, sd_v, snd, rcv, rcv_two, snd_far, rcv_far, part, relay, got1, half_sum, got2, part_far, relay_far, got_far, sum_far, got_home,
     load_sem, z_send, z_recv, y_send, y_recv, r0_send, r0_recv, r1_send, r1_recv, r2_send, r2_recv,
     f_send, f_recv, g_send, g_recv, a_send, a_recv,
@@ -404,8 +417,19 @@
             load(i, which).start()
         return carry
 
-    lax.fori_loop(0, pairs, start_loads, 0)
+    brought = [
+        pltpu.make_async_copy(src, dst, in_sem.at[k])
+        for k, (src, dst) in enumerate(((h_in, h), (hs_in, hs), (comb_in, comb), (comb_far_in, comb_far)))
+    ]
+    brought[0].start()
+    load(0, 0).start()
+    load(0, 1).start()
+    for copy in brought[1:]:
+        copy.start()
+    lax.fori_loop(1, pairs, start_loads, 0)
     here.greet()
+    for copy in brought:
+        copy.wait()
 
     def lead(half):
         return ("y", "x") if half == 0 else ("x", "y")
@@ -658,7 +682,7 @@
             held(1024, 256, dtype=F32),
             pltpu.SemaphoreType.DMA((4, pairs)),
             *both(4, 3), *both(n, 3), *both(n, 2), *both(n, 2),
-            *both(n), *both(n, 3), *both(n, 5), *both(n, 7),
+            *both(n), *both(n, 2), *both(n, 2), *both(n, 5), *both(n, 7),
         ],
         compiler_params=pltpu.CompilerParams(
             collective_id=0, has_side_effects=True, vmem_limit_bytes=60 * 2**20
@@ -668,9 +692,14 @@
     return pl.pallas_call(
         functools.partial(return_kernel, pairs),
         out_shape=jax.ShapeDtypeStruct((64, width), BF16),
-        in_specs=[vmem] * 4 + [hbm] * 2,
+        in_specs=[hbm] * 6,
         out_specs=vmem,
         scratch_shapes=[
+            held(1024, 1024),
+            held(1024, 128),
+            held(4, 256, 256),
+            held(256, 256),
+            pltpu.SemaphoreType.DMA((4,)),
             held(pairs, 1024, 2 * W),
             held(pairs, 128, 2 * W),
             held(n, 5, 128, W),

time: 178 us -> 175 us (0.983)
  Pallas kernels: 176 us -> 173 us
    pallas_call x1, Pallas kernels: 80.4 us -> 78.4 us  [shards(): pl.pallas_call(functools.partial(return_kernel, pairs), out_shape=jax.Sha...]
where the time goes in v4:
time: 175 us; the launch traced here: 174 us
  Pallas kernels  173 us (99%)
  local copies, waits for them, and re-layouts  1.82 us (1%)
    pallas_call x1, Pallas kernels, shards(): pl.pallas_call(functools.partial(dispatch_kernel, pairs), out_shape=(jax....  94.3 us
    pallas_call x1, Pallas kernels, shards(): pl.pallas_call(functools.partial(return_kernel, pairs), out_shape=jax.Sha...  78.4 us

profile of v4, /device:TPU:1, one launch (start us, length us, event | category | flops | bytes accessed | tf_op | source)
XLA Modules:
  0.0 174.5 jit_solution(16822370244575849838)
XLA Ops:
  0.0 94.3 %dispatch.1 = (bf16[1024,1024]{1,0:T(8,128)(2,1)}, bf16[1024,128]{1,0:T(8,128)(2,1)}, bf16[4,256,256]{2,1,0:T(8,128)(2,1)}, bf16[256,256]{1,0:T(8,128)(2,1)}) custom-call(bf16[64,3584]{1,0:T(8,128)(2,1)} %tok.1, s32[8,64]{1,0:T(8,128)} %bitcast.2, bf16[8,64]{1,0:T(8,128)(2,1)} %bitcast.3, bf16[1,3584,1024]{2,1,0:T(8,128)(2,1)} %w_gate.1, ...), custom_call_target="tpu_custom_call" | custom-call | tf_op jit(solution)/shard_map/dispatch/pallas_call | solution.py:655
  94.3 78.4 %bring_back.1 = bf16[64,3584]{1,0:T(8,128)(2,1)} custom-call(bf16[1024,1024]{1,0:T(8,128)(2,1)} %get-tuple-element.9.h_in, bf16[1024,128]{1,0:T(8,128)(2,1)} %get-tuple-element.10.hs_in, bf16[4,256,256]{2,1,0:T(8,128)(2,1)} %get-tuple-element.11.comb_in, bf16[256,256]{1,0:T(8,128)(2,1)} %get-tuple-element.12.comb_far_in, bf16[1,1024,3584]{2,1,0:T(8,128)(2,1)} %w_down.1, ...), custom_call_target="tpu_custom_call" | custom-call | tf_op jit(solution)/shard_map/bring_back/pallas_call | solution.py:692
  172.7 1.8 %copy.11 = bf16[64,3584]{1,0:T(8,128)(2,1)} copy(bf16[64,3584]{1,0:T(8,128)(2,1)} %bring_back.1) | data formatting | bytes 917504
